TPU v7x, 768 devices: a whole 4x8x12 slice. The times are simulated.
768 devices in a mesh: batch: 16 (over x, y_lo), proto: 48 (over y_hi, z, core).
Axes of the slice: x: 4, y: 8 (y_hi: 2, y_lo: 4; y = y_hi * 4 + y_lo), z: 12, core: 2. Of those that a mesh axis runs over, the one named last changes fastest.
Arguments:
- features: bfloat16 [8192, 256], P('batch'), may hold values from -6 to 6
- prototypes: bfloat16 [98304, 256], P(('proto', 'batch')), may hold values from -6 to 6
Outputs:
- assignments: bfloat16 [8192, 98304], P('batch', 'proto')
All inputs are finite; a program needn't handle non-finite values.
Results may differ from a plain program's by a relative error of at most 0.0061.
Values may be sent and summed in bfloat16 or wider, within the bound.
A program may use at most 32 MiB of HBM per device.

v0:
```python
import jax
import jax.numpy as jnp
from jax import lax
from jax.sharding import PartitionSpec as P

ITERS = 3


def unit_rows(matrix):
    values = matrix.astype(jnp.float32)
    scale = lax.rsqrt(1e-06 + jnp.sum(values * values, axis=1, keepdims=True))
    return (values * scale).astype(jnp.bfloat16)


def proto_sums(partial_value):
    return lax.psum(partial_value, "batch")


def image_sums(partial_value):
    return lax.psum(partial_value, "proto")


def local(features, prototypes):
    unit_feat = unit_rows(features)
    scores = jnp.einsum(
        "bd,kd->bk",
        unit_feat,
        unit_rows(lax.all_gather(prototypes, "batch", axis=0, tiled=True)),
        preferred_element_type=jnp.float32,
    )
    weights = jnp.exp(20.0 * scores)
    total_protos = float(weights.shape[1] * lax.axis_size("proto"))
    row_factor = jnp.ones((weights.shape[0],), jnp.float32)
    col_factor = jnp.ones((weights.shape[1],), jnp.float32)
    for step in range(ITERS):
        column_part = jnp.dot(row_factor, weights, precision=lax.Precision.HIGHEST)
        col_factor = 1.0 / proto_sums(column_part)
        row_part = jnp.dot(weights, col_factor, precision=lax.Precision.HIGHEST)
        row_factor = 1.0 / image_sums(row_part)
    scaled = weights * row_factor[:, None] * (total_protos * col_factor)[None, :]
    return scaled.astype(jnp.bfloat16)


def solution(mesh):
    in_specs = (P("batch", None), P(("proto", "batch"), None))
    out_specs = P("batch", "proto")
    return jax.shard_map(local, mesh=mesh, in_specs=in_specs, out_specs=out_specs, check_vma=False)
```

profile of v0, /device:TPU:1, one launch (start us, length us, event | category | flops | bytes accessed | tf_op | source)
XLA Modules:
  0.0 650.3 jit_solution(12678465682431077296)
XLA Ops:
  6.5 0.0 all-gather.2.cloned.1.call-start
  6.5 0.7 all-gather.2.cloned.1.call-update
  7.3 1.1 fusion.4
  8.4 87.2 %all-gather.2.cloned.1.call-done = bf16[2048,256]{1,0:T(8,128)(2,1)} async-done(((bf16[128,256]{1,0:T(8,128)(2,1)}), bf16[2048,256]{1,0:T(8,128)(2,1)}) %all-gather.2.cloned.1.call-update) | async-done | bytes 1048592 | tf_op jit(solution)/shard_map/all_gather | solution.py:28
  95.6 1.6 fusion
  97.2 2.2 multiply_exponential_fusion
  99.4 0.0 copy-start
  99.4 1.9 copy-done
  101.3 2.1 fusion.8
  103.4 36.0 %psum.42 = f32[2048]{0:T(1024)S(1)} all-reduce(f32[2048]{0:T(1024)S(1)} %bitcast.27), channel_id=1, replica_groups=mesh['batch'=16,'proto'=48] {'batch'}, use_global_device_ids=true, to_apply=%region_2.0 | all-reduce | flops 2048 | bytes 16384 | tf_op jit(solution)/shard_map/psum | solution.py:16
  139.5 5.8 fusion.11
  145.2 142.9 %psum.43 = f32[512]{0:T(512)S(1)} all-reduce(f32[512]{0:T(512)S(1)} %bitcast.28), channel_id=1, replica_groups=mesh['batch'=16,'proto'=48] {'proto'}, use_global_device_ids=true, to_apply=%region_3.0 | all-reduce | flops 512 | bytes 4096 | tf_op jit(solution)/shard_map/psum | solution.py:20
  288.2 4.3 fusion.12
  292.5 32.2 %psum.44 = f32[2048]{0:T(1024)S(1)} all-reduce(f32[2048]{0:T(1024)S(1)} %bitcast.24), channel_id=1, replica_groups=mesh['batch'=16,'proto'=48] {'batch'}, use_global_device_ids=true, to_apply=%region_4.0 | all-reduce | flops 2048 | bytes 16384 | tf_op jit(solution)/shard_map/psum | solution.py:16
  324.7 5.8 fusion.13
  330.5 132.3 %psum.45 = f32[512]{0:T(512)S(1)} all-reduce(f32[512]{0:T(512)S(1)} %bitcast.30), channel_id=1, replica_groups=mesh['batch'=16,'proto'=48] {'proto'}, use_global_device_ids=true, to_apply=%region_5.0 | all-reduce | flops 512 | bytes 4096 | tf_op jit(solution)/shard_map/psum | solution.py:20
  462.8 4.3 fusion.14
  467.1 33.7 %psum.46 = f32[2048]{0:T(1024)S(1)} all-reduce(f32[2048]{0:T(1024)S(1)} %bitcast.26), channel_id=1, replica_groups=mesh['batch'=16,'proto'=48] {'batch'}, use_global_device_ids=true, to_apply=%region_6.0 | all-reduce | flops 2048 | bytes 16384 | tf_op jit(solution)/shard_map/psum | solution.py:16
  500.8 5.8 fusion.15
  506.6 132.9 %psum.47 = f32[512]{0:T(512)S(1)} all-reduce(f32[512]{0:T(512)S(1)} %bitcast.32), channel_id=1, replica_groups=mesh['batch'=16,'proto'=48] {'proto'}, use_global_device_ids=true, to_apply=%region_7.0 | all-reduce | flops 512 | bytes 4096 | tf_op jit(solution)/shard_map/psum | solution.py:20
  639.5 3.9 multiply_convert_fusion
  (8 shorter events, 0.0 us)
Async XLA Ops:
  6.5 89.1 %all-gather.2.cloned.1.call-start = ((), (), s32[]{:S(2)}) async-start(), calls=%async_computation | async-start | bytes 1114112 | tf_op jit(solution)/shard_map/all_gather | solution.py:28
  99.4 1.9 copy-start
Sparse Core Ops, SparseCore 0:
  9.7 85.8 all-gather.1
where the time goes:
time: 651 us; the launch traced here: 650 us
  blocking collectives  510 us (78%)
  waiting for transfers between devices  87.9 us (14%)
  matrix products  30.1 us (5%)
  between operations  13.5 us (2%)
  other arithmetic  6.63 us (1%)
    psum x3, blocking collectives, image_sums(): return lax.psum(partial_value, 'proto')  408 us
    psum x3, blocking collectives, proto_sums(): return lax.psum(partial_value, 'batch')  102 us
    all_gather x1, waiting for transfers between devices, local(): lax.all_gather(prototypes, 'batch', axis=0, tiled=True)  87.2 us
    dot_general x3, matrix products, local(): row_part = jnp.dot(weights, col_factor, precision=lax.Precision.HIGHEST)  17.3 us
  transfers between devices with their start and end apart: 1, of which 1 were waited for; matrix products, arithmetic and copies ran while one was open for 0% of the time, Pallas kernels for 0%

commit v1 on v0

v1 whole, which is shorter than its diff:
```python
import jax
import jax.numpy as jnp
from jax import lax
from jax.experimental import pallas as pl
from jax.experimental.pallas import tpu as pltpu
from jax.sharding import PartitionSpec as P

ITERS = 3
NX, NY, NZ = 4, 4, 12
ROWS, COLS, DEPTH, BLOCK = 512, 2048, 256, 128
TOTAL_PROTOS = 98304.0
MESH = pl.DeviceIdType.MESH
NT = (((1,), (1,)), ((), ()))


def unit_rows(values):
    values = values.astype(jnp.float32)
    scale = lax.rsqrt(1e-06 + jnp.sum(values * values, axis=1, keepdims=True))
    return (values * scale).astype(jnp.bfloat16)


def split(values):
    high = values.astype(jnp.bfloat16)
    low = (values - high.astype(jnp.float32)).astype(jnp.bfloat16)
    return high, low


def kernel(
    feat_ref, proto_ref, scaled_ref, row_ref,
    blocks, unit_feat, weights,
    col_own, col_x, col_y, row_own, row_a, row_z,
    y_send, y_recv, x_send, x_recv, f_send, f_recv,
    cx_send, cx_recv, cy_send, cy_recv, ra_send, ra_recv, rz_send, rz_recv,
):
    batch, proto = lax.axis_index("batch"), lax.axis_index("proto")
    x, y = batch // NY, batch % NY
    yh, z, core = proto // (2 * NZ), (proto // 2) % NZ, proto % 2
    xs = [lax.rem(x + d, NX) for d in range(NX)]
    ys = [y, y + 1 - 2 * lax.rem(y, 2), lax.rem(y + 2, NY), NY - 1 - y]
    near = [(yh, 1 - core), (1 - yh, core), (1 - yh, 1 - core)]
    zs = [lax.rem(z + d, NZ) for d in range(NZ)]

    def at(px, py):
        return {"batch": px * NY + py, "proto": proto}

    def over(pyh, pz, pcore):
        return {"batch": batch, "proto": (pyh * NZ + pz) * 2 + pcore}

    barrier = pltpu.get_barrier_semaphore()
    partners = [at(px, y) for px in xs[1:]] + [at(x, py) for py in ys[1:]]
    partners += [over(a, z, b) for a, b in near] + [over(yh, pz, core) for pz in zs[1:]]
    for partner in partners:
        pl.semaphore_signal(barrier, inc=1, device_id=partner, device_id_type=MESH)
    blocks[batch] = unit_rows(proto_ref[...])
    unit_feat[...] = unit_rows(feat_ref[...])
    pl.semaphore_wait(barrier, len(partners))

    def remote(src, dst, send, recv, device):
        copy = pltpu.make_async_remote_copy(
            src_ref=src, dst_ref=dst, send_sem=send, recv_sem=recv,
            device_id=device, device_id_type=MESH,
        )
        copy.start()
        return copy

    sent = []

    def compute(index):
        scores = lax.dot_general(
            unit_feat[...], blocks[index], NT, preferred_element_type=jnp.float32
        )
        columns = pl.ds(pl.multiple_of(index * BLOCK, BLOCK), BLOCK)
        weights[:, columns] = jnp.exp(20.0 * scores).astype(jnp.bfloat16)

    right, left, across = xs[1], xs[3], xs[2]
    half = BLOCK // 2
    x_copies, f_copies = {}, {}

    def spread(k):
        block = blocks.at[x * NY + ys[k]]
        x_copies[k] = [
            remote(block, block, x_send.at[k, 0], x_recv.at[k, 0], at(right, y)),
            remote(block, block, x_send.at[k, 1], x_recv.at[k, 1], at(left, y)),
        ]
        sent.extend(x_copies[k])

    def forward(k):
        x_copies[k][0].wait_recv()
        block = blocks.at[left * NY + ys[k], pl.ds(0, half)]
        first = remote(block, block, f_send.at[k, 0], f_recv.at[k, 0], at(right, y))
        x_copies[k][1].wait_recv()
        block = blocks.at[right * NY + ys[k], pl.ds(half, half)]
        second = remote(block, block, f_send.at[k, 1], f_recv.at[k, 1], at(left, y))
        f_copies[k] = [first, second]
        sent.extend(f_copies[k])
        compute(left * NY + ys[k])
        compute(right * NY + ys[k])

    def finish(k):
        for copy in f_copies[k]:
            copy.wait_recv()
        compute(across * NY + ys[k])

    spread(0)
    own = blocks.at[batch]
    y_copies = [
        remote(own, own, y_send.at[k - 1], y_recv.at[k - 1], at(x, ys[k])) for k in range(1, NY)
    ]
    sent.extend(y_copies)
    compute(batch)
    for k in range(1, NY):
        y_copies[k - 1].wait_recv()
        spread(k)
        forward(k - 1)
        compute(x * NY + ys[k])
        if k > 1:
            finish(k - 2)
    forward(NY - 1)
    finish(NY - 2)
    finish(NY - 1)

    col_mask = lax.broadcasted_iota(jnp.int32, (8, COLS), 1) // 256 == lax.broadcasted_iota(
        jnp.int32, (8, COLS), 0
    )
    row_of = lax.broadcasted_iota(jnp.int32, (8, 256), 0)
    row_factor = [jnp.ones((1, BLOCK), jnp.float32)] * 4
    for step in range(ITERS):
        wide = jnp.concatenate([jnp.broadcast_to(part, (8, BLOCK)) for part in row_factor], axis=1)
        if step:
            high, low = split(wide)
            summed = jnp.dot(high, weights[...], preferred_element_type=jnp.float32)
            summed += jnp.dot(low, weights[...], preferred_element_type=jnp.float32)
        else:
            summed = jnp.dot(
                wide.astype(jnp.bfloat16), weights[...], preferred_element_type=jnp.float32
            )
        part = jnp.zeros((8, 256), jnp.float32)
        for k in range(8):
            part = jnp.where(row_of == k, summed[:, k * 256:(k + 1) * 256], part)

        def exchange(value, mine, slots, send, recv, devices):
            mine[...] = value
            copies = [
                remote(mine, slots.at[i], send.at[i], recv.at[i], device)
                for i, device in enumerate(devices)
            ]
            sent.extend(copies)
            total = value
            for i, copy in enumerate(copies):
                copy.wait_recv()
                total = total + slots[i]
            return total

        part = exchange(
            part, col_own.at[step, 0], col_x.at[step], cx_send.at[step], cx_recv.at[step],
            [at(px, y) for px in xs[1:]],
        )
        part = exchange(
            part, col_own.at[step, 1], col_y.at[step], cy_send.at[step], cy_recv.at[step],
            [at(x, py) for py in ys[1:]],
        )
        col_factor = 1.0 / part
        tiled = jnp.where(col_mask, jnp.concatenate([col_factor] * 8, axis=1), 0.0)
        high, low = split(tiled)
        rows = lax.dot_general(high, weights[...], NT, preferred_element_type=jnp.float32)
        rows += lax.dot_general(low, weights[...], NT, preferred_element_type=jnp.float32)
        rows = jnp.sum(rows, axis=0, keepdims=True)
        part = jnp.concatenate([rows[:, k * BLOCK:(k + 1) * BLOCK] for k in range(4)], axis=0)
        part = exchange(
            part, row_own.at[step, 0], row_a.at[step], ra_send.at[step], ra_recv.at[step],
            [over(a, z, b) for a, b in near],
        )
        if step == ITERS - 1:
            flat = jnp.sum(tiled, axis=0, keepdims=True) * TOTAL_PROTOS
            scaled_ref[...] = (weights[...].astype(jnp.float32) * flat).astype(jnp.bfloat16)
        part = exchange(
            part, row_own.at[step, 1], row_z.at[step], rz_send.at[step], rz_recv.at[step],
            [over(yh, pz, core) for pz in zs[1:]],
        )
        result = 1.0 / part
        row_factor = [result[k:k + 1] for k in range(4)]
    row_ref[...] = result
    for copy in sent:
        copy.wait_send()


def local(features, prototypes):
    vmem = pl.BlockSpec(memory_space=pltpu.VMEM)
    dma = pltpu.SemaphoreType.DMA
    scaled, rows = pl.pallas_call(
        kernel,
        out_shape=(
            jax.ShapeDtypeStruct((ROWS, COLS), jnp.bfloat16),
            jax.ShapeDtypeStruct((4, BLOCK), jnp.float32),
        ),
        in_specs=[vmem, vmem],
        out_specs=(vmem, vmem),
        scratch_shapes=[
            pltpu.VMEM((NX * NY, BLOCK, DEPTH), jnp.bfloat16),
            pltpu.VMEM((ROWS, DEPTH), jnp.bfloat16),
            pltpu.VMEM((ROWS, COLS), jnp.bfloat16),
            pltpu.VMEM((ITERS, 2, 8, 256), jnp.float32),
            pltpu.VMEM((ITERS, 3, 8, 256), jnp.float32),
            pltpu.VMEM((ITERS, 3, 8, 256), jnp.float32),
            pltpu.VMEM((ITERS, 2, 4, BLOCK), jnp.float32),
            pltpu.VMEM((ITERS, 3, 4, BLOCK), jnp.float32),
            pltpu.VMEM((ITERS, NZ - 1, 4, BLOCK), jnp.float32),
            dma((3,)), dma((3,)), dma((4, 2)), dma((4, 2)), dma((4, 2)), dma((4, 2)),
            dma((ITERS, 3)), dma((ITERS, 3)), dma((ITERS, 3)), dma((ITERS, 3)),
            dma((ITERS, 3)), dma((ITERS, 3)), dma((ITERS, NZ - 1)), dma((ITERS, NZ - 1)),
        ],
        compiler_params=pltpu.CompilerParams(collective_id=0, has_side_effects=True),
    )(features, prototypes)
    return (scaled.astype(jnp.float32) * rows.reshape(ROWS)[:, None]).astype(jnp.bfloat16)


def solution(mesh):
    in_specs = (P("batch", None), P(("proto", "batch"), None))
    out_specs = P("batch", "proto")
    return jax.shard_map(local, mesh=mesh, in_specs=in_specs, out_specs=out_specs, check_vma=False)
```

time: 651 us -> 101 us (0.16)
  blocking collectives: 510 us -> 0 us
  Pallas kernels: 0 us -> 98 us
  waiting for transfers between devices: 87.9 us -> 0 us
  matrix products: 30.1 us -> 0 us
  between operations: 13.5 us -> 0.01 us
    psum x6 -> x0, blocking collectives: 510 us -> none  [the longest x3 408 us: image_sums(): return lax.psum(partial_value, 'proto')]
    pallas_call x0 -> x1, Pallas kernels: none -> 98 us  [local(): pl.pallas_call(kernel, out_shape=(jax.ShapeDtypeStruct((ROWS, COLS), jnp....]
    all_gather x1 -> x0, waiting for transfers between devices: 87.2 us -> none  [local(): lax.all_gather(prototypes, 'batch', axis=0, tiled=True)]
    dot_general x7 -> x0, matrix products: 30.1 us -> none  [the longest x3 17.3 us: local(): row_part = jnp.dot(weights, col_factor, precision=lax.Precision.HIGHEST)]
  transfers between devices with their start and end apart: 1 -> 0, of which waited for: 1 -> 0; matrix products, arithmetic and copies ran while one was open for 0% -> 0% of each run, Pallas kernels for 0% -> 0%
where the time goes in v1:
time: 101 us
  Pallas kernels  98 us (97%)
  other arithmetic  3.32 us (3%)
    pallas_call x1, Pallas kernels, local(): pl.pallas_call(kernel, out_shape=(jax.ShapeDtypeStruct((ROWS, COLS), jnp....  98 us
    convert_element_type x1, other arithmetic, local(): (scaled.astype(jnp.float32) * rows.reshape(ROWS)[:, None]).astype(jnp.bfl...  3.32 us

profile of v1, /device:TPU:1, one launch (start us, length us, event | category | flops | bytes accessed | tf_op | source)
XLA Modules:
  0.0 101.3 jit_solution(6773097106822724549)
XLA Ops:
  0.0 98.0 %shard_map.28 = (bf16[512,2048]{1,0:T(8,128)(2,1)}, f32[4,128]{1,0:T(4,128)}) custom-call(bf16[512,256]{1,0:T(8,128)(2,1)} %feat_ref.1, bf16[128,256]{1,0:T(8,128)(2,1)} %proto_ref.1), custom_call_target="tpu_custom_call" | custom-call | tf_op jit(solution)/shard_map/pallas_call | solution.py:190
  98.0 3.3 %multiply_convert_fusion = bf16[512,2048]{1,0:T(8,128)(2,1)} fusion(bf16[512,2048]{1,0:T(8,128)(2,1)} %get-tuple-element.7, f32[512]{0:T(512)} %bitcast.1), kind=kLoop, calls=%fused_computation | loop fusion | flops 3145728 | bytes 4196352 | tf_op jit(solution)/shard_map/convert_element_type | solution.py:214

commit v2 on v0

v2 whole, which is shorter than its diff:
```python
import jax
import jax.numpy as jnp
from jax import lax
from jax.experimental import pallas as pl
from jax.experimental.pallas import tpu as pltpu
from jax.sharding import PartitionSpec as P

ITERS = 3
NX, NY, NZ, RING = 4, 4, 12, 8
ROWS, COLS, DEPTH, BLOCK = 512, 2048, 256, 128
TILE, HALF = 1024, 256
TOTAL_PROTOS = 98304.0
MESH = pl.DeviceIdType.MESH
NT = (((1,), (1,)), ((), ()))
F32, BF16 = jnp.float32, jnp.bfloat16


def unit_rows(values):
    values = values.astype(F32)
    scale = lax.rsqrt(1e-06 + jnp.sum(values * values, axis=1, keepdims=True))
    return (values * scale).astype(BF16)


def split(values):
    high = values.astype(BF16)
    low = (values - high.astype(F32)).astype(BF16)
    return jnp.concatenate([high, low], axis=0)


def kernel(
    feat_ref, proto_ref, scaled_ref, row_ref,
    own_feat, feats, protos, other, weights,
    col_own, col_in, ring_own, ring_in, z_own, z_in, last_own, last_in, lastz_own, lastz_in, col_last,
    fs, fr, ps, pr, gs, gr, cs, cr, ys, yr, zs, zr, ls, lr, lzs, lzr, bs, br, es, er, hs, hr, ks, kr,
):
    batch, proto = lax.axis_index("batch"), lax.axis_index("proto")
    x, yl = batch // NY, lax.rem(batch, NY)
    yh, z, core = proto // (2 * NZ), lax.rem(proto // 2, NZ), lax.rem(proto, 2)
    y = yh * NY + yl
    mate = 1 - core

    def device(px, py, pz, pcore):
        return {
            "batch": px * NY + lax.rem(py, NY),
            "proto": ((py // NY) * NZ + pz) * 2 + pcore,
        }

    xs = [lax.rem(x + d, NX) for d in range(NX)]
    ry = [lax.rem(y + d, RING) for d in range(RING)]
    rz = [lax.rem(z + d, NZ) for d in range(NZ)]
    near_y = [yl, yl + 1 - 2 * lax.rem(yl, 2), lax.rem(yl + 2, NY), NY - 1 - yl]
    col_peers = [device(px, y, z, core) for px in xs[1:]] + [device(px, y, z, mate) for px in xs]
    ring_peers = [device(x, py, z, core) for py in ry[1:]]
    last_peers = [(py, device(x, py, z, core)) for py in ry[1:]]
    last_peers += [(py, device(x, py, z, mate)) for py in ry]
    z_peers = [device(x, y, pz, core) for pz in rz[1:]]

    barrier = pltpu.get_barrier_semaphore()
    partners = col_peers + [peer for _, peer in last_peers if peer is not last_peers[7][1]] + z_peers
    for partner in partners:
        pl.semaphore_signal(barrier, inc=1, device_id=partner, device_id_type=MESH)
    protos[batch] = unit_rows(proto_ref[...])
    own_feat[...] = unit_rows(feat_ref[...])
    mine = pl.ds(pl.multiple_of(core * HALF, HALF), HALF)
    feats[yl] = own_feat[mine, :]
    pl.semaphore_wait(barrier, len(partners))

    sent = []

    def remote(src, dst, send, recv, peer):
        copy = pltpu.make_async_remote_copy(
            src_ref=src, dst_ref=dst, send_sem=send, recv_sem=recv,
            device_id=peer, device_id_type=MESH,
        )
        copy.start()
        sent.append(copy)
        return copy

    block = protos.at[batch]
    proto_copies = [
        remote(block, block, ps.at[d - 1], pr.at[d - 1], device(xs[d], y, z, core)) for d in (1, 3, 2)
    ]
    feat_copies = [
        remote(own_feat.at[mine], feats.at[yl], fs.at[0], fr.at[0], device(x, ry[1], z, core)),
        remote(own_feat.at[mine], feats.at[yl], fs.at[1], fr.at[1], device(x, ry[7], z, core)),
    ]
    for i, py in enumerate((ry[2], ry[6])):
        src = own_feat.at[pl.ds(pl.multiple_of(core * HALF + i * BLOCK, BLOCK), BLOCK)]
        dst = feats.at[yl, pl.ds(i * BLOCK, BLOCK)]
        feat_copies.append(remote(src, dst, fs.at[2 + i], fr.at[2 + i], device(x, py, z, core)))
    partner = device(x, y, z, mate)
    mate_copies = [remote(block, other.at[x], gs.at[0], gr.at[0], partner)]

    def fill(row_block, columns, image, vectors, count):
        scores = lax.dot_general(image, vectors, NT, preferred_element_type=F32)
        rows = pl.ds(pl.multiple_of(row_block * BLOCK, BLOCK), count)
        weights[rows, pl.ds(pl.multiple_of(columns * BLOCK, BLOCK), BLOCK)] = jnp.exp(
            20.0 * scores
        ).astype(BF16)

    def fill_images(row_block, image, count):
        for px in range(NX):
            fill(row_block, core * NX + px, image, protos[px * NY + yl], count)
            fill(row_block, mate * NX + px, image, other[px], count)

    for slot, (copy, d) in enumerate(zip(proto_copies, (3, 1, 2))):
        copy.wait_recv()
        arrived = protos.at[xs[d] * NY + yl]
        mate_copies.append(
            remote(arrived, other.at[xs[d]], gs.at[1 + slot], gr.at[1 + slot], partner)
        )
    for copy in mate_copies:
        copy.wait_recv()
    fill_images(yl * 2, feats[yl], HALF)
    for copy, shift in zip(feat_copies[:2], (3, 1)):
        copy.wait_recv()
        source = lax.rem(yl + shift, NY)
        fill_images(source * 2, feats[source], HALF)
    source = lax.rem(yl + 2, NY)
    for i, copy in enumerate(feat_copies[2:]):
        copy.wait_recv()
        fill_images(source * 2 + i, feats[source, i * BLOCK:(i + 1) * BLOCK], BLOCK)

    tile_mask = lax.broadcasted_iota(jnp.int32, (8, TILE), 1) // BLOCK == lax.broadcasted_iota(
        jnp.int32, (8, TILE), 0
    )
    row_of = lax.broadcasted_iota(jnp.int32, (8, BLOCK), 0)

    def fold(wide):
        part = wide[:, :BLOCK]
        for k in range(1, 8):
            part = jnp.where(row_of == k, wide[:, k * BLOCK:(k + 1) * BLOCK], part)
        return part

    def column_sums(factor):
        wide = jnp.concatenate(
            [jnp.broadcast_to(factor[k:k + 1], (8, BLOCK)) for k in range(8)], axis=1
        )
        summed = jnp.dot(split(wide), weights[...], preferred_element_type=F32)
        return fold(summed[:8] + summed[8:])

    def row_sums(factor):
        wide = jnp.where(tile_mask, jnp.concatenate([factor] * 8, axis=1), 0.0)
        summed = lax.dot_general(split(wide), weights[...], NT, preferred_element_type=F32)
        return fold(jnp.broadcast_to(jnp.sum(summed, axis=0, keepdims=True), (8, TILE)))

    def start(value, own, slots, send, recv, peers):
        own[...] = value.astype(own.dtype)
        return [remote(own, slots.at[i], send.at[i], recv.at[i], peer) for i, peer in enumerate(peers)]

    def finish(total, slots, copies):
        for i, copy in enumerate(copies):
            copy.wait_recv()
            total = total + slots[i].astype(F32)
        return total

    half = BLOCK // 2
    row_factor = jnp.ones((8, BLOCK), F32)
    for step in range(ITERS):
        part = column_sums(row_factor)
        copies = start(part, col_own.at[step], col_in.at[step], cs.at[step], cr.at[step], col_peers)
        part = finish(part, col_in.at[step], copies)
        col_factor = 1.0 / part
        if step == 1:
            for copy in y_copies:
                copy.wait_recv()
            x_copies = []
            for k in range(1, NY):
                block = protos.at[x * NY + near_y[k]]
                for side, d in enumerate((1, 3)):
                    x_copies.append(
                        remote(block, block, es.at[k - 1, side], er.at[k - 1, side], device(xs[d], y, z, core))
                    )
        part = row_sums(col_factor)
        if step == ITERS - 1:
            last_col = jnp.where(core == 0, col_factor[:4], col_factor[4:]) * TOTAL_PROTOS
            col_last[yl] = last_col
            for k in range(4):
                last_own[k] = part[2 * k:2 * k + 2]
            copies = [
                remote(last_own.at[lax.rem(py, NY)], last_in.at[i], ls.at[i], lr.at[i], peer)
                for i, (py, peer) in enumerate(last_peers)
            ]
            k_copies = [
                remote(col_last.at[yl], col_last.at[yl], ks.at[k - 1], kr.at[k - 1],
                       device(x, yh * NY + near_y[k], z, core))
                for k in range(1, NY)
            ]
            mine_sum = last_own[yl]
            mate_sum = jnp.zeros((2, BLOCK), F32)
            for i, copy in enumerate(copies):
                copy.wait_recv()
                if i < 7:
                    mine_sum = mine_sum + last_in[i]
                else:
                    mate_sum = mate_sum + last_in[i]
            first = jnp.where(core == 0, mine_sum, mate_sum)
            second = jnp.where(core == 0, mate_sum, mine_sum)
            part = jnp.concatenate([first, second], axis=0)
            copies = start(part, lastz_own, lastz_in, lzs, lzr, z_peers)
            for copy in f_copies:
                copy.wait_recv()
            for copy in k_copies:
                copy.wait_recv()
            for b in range(NX * NY):
                scores = lax.dot_general(own_feat[...], protos[b], NT, preferred_element_type=F32)
                factor = col_last[b % NY, b // NY:b // NY + 1, :]
                scaled_ref[:, b * BLOCK:(b + 1) * BLOCK] = jnp.exp(20.0 * scores) * factor
            row_ref[...] = 1.0 / finish(part, lastz_in, copies)
            break
        copies = start(part, ring_own.at[step], ring_in.at[step], ys.at[step], yr.at[step], ring_peers)
        part = finish(part, ring_in.at[step], copies)
        copies = start(part, z_own.at[step], z_in.at[step], zs.at[step], zr.at[step], z_peers)
        if step == 0:
            block = protos.at[batch]
            y_copies = [
                remote(block, block, bs.at[k - 1], br.at[k - 1], device(x, yh * NY + near_y[k], z, core))
                for k in range(1, NY)
            ]
        else:
            f_copies = []
            for k in range(1, NY):
                for side, (source, d) in enumerate(((xs[3], 1), (xs[1], 3))):
                    x_copies[2 * (k - 1) + side].wait_recv()
                    piece = protos.at[source * NY + near_y[k], pl.ds(side * half, half)]
                    f_copies.append(
                        remote(piece, piece, hs.at[k - 1, side], hr.at[k - 1, side], device(xs[d], y, z, core))
                    )
        row_factor = 1.0 / finish(part, z_in.at[step], copies)
    for copy in sent:
        copy.wait_send()


def local(features, prototypes):
    vmem = pl.BlockSpec(memory_space=pltpu.VMEM)
    dma = pltpu.SemaphoreType.DMA
    early = ITERS - 1
    scaled, rows = pl.pallas_call(
        kernel,
        out_shape=(
            jax.ShapeDtypeStruct((ROWS, COLS), F32),
            jax.ShapeDtypeStruct((4, BLOCK), F32),
        ),
        in_specs=[vmem, vmem],
        out_specs=(vmem, vmem),
        scratch_shapes=[
            pltpu.VMEM((ROWS, DEPTH), BF16),
            pltpu.VMEM((NY, HALF, DEPTH), BF16),
            pltpu.VMEM((NX * NY, BLOCK, DEPTH), BF16),
            pltpu.VMEM((NX, BLOCK, DEPTH), BF16),
            pltpu.VMEM((TILE, TILE), BF16),
            pltpu.VMEM((ITERS, 8, BLOCK), BF16),
            pltpu.VMEM((ITERS, 7, 8, BLOCK), BF16),
            pltpu.VMEM((early, 8, BLOCK), BF16),
            pltpu.VMEM((early, 7, 8, BLOCK), BF16),
            pltpu.VMEM((early, 8, BLOCK), BF16),
            pltpu.VMEM((early, 11, 8, BLOCK), BF16),
            pltpu.VMEM((NY, 2, BLOCK), F32),
            pltpu.VMEM((15, 2, BLOCK), F32),
            pltpu.VMEM((4, BLOCK), F32),
            pltpu.VMEM((11, 4, BLOCK), F32),
            pltpu.VMEM((NY, NX, BLOCK), F32),
            dma((4,)), dma((4,)), dma((3,)), dma((3,)), dma((4,)), dma((4,)),
            dma((ITERS, 7)), dma((ITERS, 7)), dma((early, 7)), dma((early, 7)),
            dma((early, 11)), dma((early, 11)), dma((15,)), dma((15,)), dma((11,)), dma((11,)),
            dma((3,)), dma((3,)), dma((3, 2)), dma((3, 2)), dma((3, 2)), dma((3, 2)), dma((3,)), dma((3,)),
        ],
        compiler_params=pltpu.CompilerParams(
            collective_id=0, has_side_effects=True, vmem_limit_bytes=24 << 20
        ),
    )(features, prototypes)
    return (scaled * rows.reshape(ROWS)[:, None]).astype(BF16)


def solution(mesh):
    in_specs = (P("batch", None), P(("proto", "batch"), None))
    out_specs = P("batch", "proto")
    return jax.shard_map(local, mesh=mesh, in_specs=in_specs, out_specs=out_specs, check_vma=False)
```

time: 651 us -> 78.2 us (0.12)
  blocking collectives: 510 us -> 0 us
  waiting for transfers between devices: 87.9 us -> 0 us
  Pallas kernels: 0 us -> 74.6 us
  matrix products: 30.1 us -> 0 us
  between operations: 13.5 us -> 0.01 us
    psum x6 -> x0, blocking collectives: 510 us -> none  [the longest x3 408 us: image_sums(): return lax.psum(partial_value, 'proto')]
    all_gather x1 -> x0, waiting for transfers between devices: 87.2 us -> none  [local(): lax.all_gather(prototypes, 'batch', axis=0, tiled=True)]
    pallas_call x0 -> x1, Pallas kernels: none -> 74.6 us  [local(): pl.pallas_call(kernel, out_shape=(jax.ShapeDtypeStruct((ROWS, COLS), F32)...]
    dot_general x7 -> x0, matrix products: 30.1 us -> none  [the longest x3 17.3 us: local(): row_part = jnp.dot(weights, col_factor, precision=lax.Precision.HIGHEST)]
  transfers between devices with their start and end apart: 1 -> 0, of which waited for: 1 -> 0; matrix products, arithmetic and copies ran while one was open for 0% -> 0% of each run, Pallas kernels for 0% -> 0%
where the time goes in v2:
time: 78.2 us; the launch traced here: 78 us
  Pallas kernels  74.6 us (95%)
  local copies, waits for them, and re-layouts  1.79 us (2%)
  other arithmetic  1.61 us (2%)
    pallas_call x1, Pallas kernels, local(): pl.pallas_call(kernel, out_shape=(jax.ShapeDtypeStruct((ROWS, COLS), F32)...  74.6 us
    unnamed x4, local copies, waits for them, and re-layouts  1.79 us
    convert_element_type x1, other arithmetic, local(): return (scaled * rows.reshape(ROWS)[:, None]).astype(BF16)  1.61 us

profile of v2, /device:TPU:1, one launch (start us, length us, event | category | flops | bytes accessed | tf_op | source)
XLA Modules:
  0.0 78.0 jit_solution(17085955658878176949)
XLA Ops:
  0.0 0.0 copy-start
  0.0 0.9 %copy-done = bf16[512,256]{1,0:T(8,128)(2,1)S(1)} copy-done((bf16[512,256]{1,0:T(8,128)(2,1)S(1)}, bf16[512,256]{1,0:T(8,128)(2,1)}, u32[]{:S(2)}) %copy-start) | copy-done | bytes 262168
  1.0 0.0 copy-start.1
  1.0 0.8 %copy-done.1 = bf16[128,256]{1,0:T(8,128)(2,1)S(1)} copy-done((bf16[128,256]{1,0:T(8,128)(2,1)S(1)}, bf16[128,256]{1,0:T(8,128)(2,1)}, u32[]{:S(2)}) %copy-start.1) | copy-done | bytes 65560
  1.8 74.6 %shard_map.28 = (f32[512,2048]{1,0:T(8,128)S(1)}, f32[4,128]{1,0:T(4,128)S(1)}) custom-call(bf16[512,256]{1,0:T(8,128)(2,1)S(1)} %copy-done, bf16[128,256]{1,0:T(8,128)(2,1)S(1)} %copy-done.1), custom_call_target="tpu_custom_call" | custom-call | tf_op jit(solution)/shard_map/pallas_call | solution.py:238
  76.4 1.6 %multiply_convert_fusion = bf16[512,2048]{1,0:T(8,128)(2,1)} fusion(f32[512,2048]{1,0:T(8,128)S(1)} %get-tuple-element.7, f32[512]{0:T(512)S(1)} %bitcast.1), kind=kLoop, calls=%fused_computation | loop fusion | flops 2097152 | bytes 6293504 | tf_op jit(solution)/shard_map/convert_element_type | solution.py:272
Async XLA Ops:
  0.0 0.9 %copy-start = (bf16[512,256]{1,0:T(8,128)(2,1)S(1)}, bf16[512,256]{1,0:T(8,128)(2,1)}, u32[]{:S(2)}) copy-start(bf16[512,256]{1,0:T(8,128)(2,1)} %feat_ref.1) | copy-start | bytes 786436
  1.0 0.8 %copy-start.1 = (bf16[128,256]{1,0:T(8,128)(2,1)S(1)}, bf16[128,256]{1,0:T(8,128)(2,1)}, u32[]{:S(2)}) copy-start(bf16[128,256]{1,0:T(8,128)(2,1)} %proto_ref.1) | copy-start | bytes 196612

commit v3 on v2

--- a/solution.py
+++ b/solution.py
@@ -29,9 +29,9 @@
 
 def kernel(
     feat_ref, proto_ref, scaled_ref, row_ref,
-    own_feat, feats, protos, other, weights,
+    loaded, own_feat, feats, unit_feats, protos, other, unit_protos, weights, across,
     col_own, col_in, ring_own, ring_in, z_own, z_in, last_own, last_in, lastz_own, lastz_in, col_last,
-    fs, fr, ps, pr, gs, gr, cs, cr, ys, yr, zs, zr, ls, lr, lzs, lzr, bs, br, es, er, hs, hr, ks, kr,
+    fs, fr, ps, pr, gs, gr, cs, cr, ys, yr, zs, zr, ls, lr, lzs, lzr, bs, br, es, er, hs, hr, ks, kr, ms, token_a, token_b,
 ):
     batch, proto = lax.axis_index("batch"), lax.axis_index("proto")
     x, yl = batch // NY, lax.rem(batch, NY)
@@ -49,20 +49,31 @@
     ry = [lax.rem(y + d, RING) for d in range(RING)]
     rz = [lax.rem(z + d, NZ) for d in range(NZ)]
     near_y = [yl, yl + 1 - 2 * lax.rem(yl, 2), lax.rem(yl + 2, NY), NY - 1 - yl]
-    col_peers = [device(px, y, z, core) for px in xs[1:]] + [device(px, y, z, mate) for px in xs]
-    ring_peers = [device(x, py, z, core) for py in ry[1:]]
-    last_peers = [(py, device(x, py, z, core)) for py in ry[1:]]
-    last_peers += [(py, device(x, py, z, mate)) for py in ry]
-    z_peers = [device(x, y, pz, core) for pz in rz[1:]]
-
+    col_peers = [device(xs[d], y, z, c) for d in (2, 1, 3) for c in (core, mate)]
+    col_peers.append(device(x, y, z, mate))
+    far_y = [ry[d] for d in (4, 3, 5, 2, 6, 1, 7)]
+    ring_peers = [device(x, py, z, core) for py in far_y]
+    last_peers = [(py, device(x, py, z, core)) for py in far_y]
+    last_peers += [(py, device(x, py, z, mate)) for py in far_y + [y]]
+    z_peers = [device(x, y, rz[d], core) for d in (6, 5, 7, 4, 8, 3, 9, 2, 10, 1, 11)]
+
+    def signal(semaphore, peers):
+        for peer in peers:
+            pl.semaphore_signal(semaphore, inc=1, device_id=peer, device_id_type=MESH)
+
+    two_y = [device(x, py, z, core) for py in (ry[2], ry[6])]
+    one_y = [device(x, py, z, core) for py in (ry[1], ry[7])]
+    two_z = [device(x, y, pz, core) for pz in (rz[2], rz[10])]
+    one_z = [device(x, y, pz, core) for pz in (rz[1], rz[11])]
     barrier = pltpu.get_barrier_semaphore()
-    partners = col_peers + [peer for _, peer in last_peers if peer is not last_peers[7][1]] + z_peers
-    for partner in partners:
-        pl.semaphore_signal(barrier, inc=1, device_id=partner, device_id_type=MESH)
-    protos[batch] = unit_rows(proto_ref[...])
-    own_feat[...] = unit_rows(feat_ref[...])
-    mine = pl.ds(pl.multiple_of(core * HALF, HALF), HALF)
-    feats[yl] = own_feat[mine, :]
+    partners = two_y + two_z + col_peers + one_y + one_z
+    signal(barrier, partners)
+    loads = [
+        pltpu.make_async_copy(feat_ref, loaded, ms.at[0]),
+        pltpu.make_async_copy(proto_ref, protos.at[batch], ms.at[1]),
+    ]
+    for load in loads:
+        load.start()
     pl.semaphore_wait(barrier, len(partners))
 
     sent = []
@@ -76,50 +87,62 @@
         sent.append(copy)
         return copy
 
-    block = protos.at[batch]
     proto_copies = [
-        remote(block, block, ps.at[d - 1], pr.at[d - 1], device(xs[d], y, z, core)) for d in (1, 3, 2)
+        remote(proto_ref, protos.at[batch], ps.at[d - 1], pr.at[d - 1], device(xs[d], y, z, core))
+        for d in (2, 1, 3)
     ]
+    mine = pl.ds(pl.multiple_of(core * HALF, HALF), HALF)
     feat_copies = [
-        remote(own_feat.at[mine], feats.at[yl], fs.at[0], fr.at[0], device(x, ry[1], z, core)),
-        remote(own_feat.at[mine], feats.at[yl], fs.at[1], fr.at[1], device(x, ry[7], z, core)),
+        remote(feat_ref.at[mine], feats.at[yl], fs.at[i], fr.at[i], peer)
+        for i, peer in enumerate(one_y)
     ]
-    for i, py in enumerate((ry[2], ry[6])):
-        src = own_feat.at[pl.ds(pl.multiple_of(core * HALF + i * BLOCK, BLOCK), BLOCK)]
+    for i, peer in enumerate(two_y):
+        src = feat_ref.at[pl.ds(pl.multiple_of(core * HALF + i * BLOCK, BLOCK), BLOCK)]
         dst = feats.at[yl, pl.ds(i * BLOCK, BLOCK)]
-        feat_copies.append(remote(src, dst, fs.at[2 + i], fr.at[2 + i], device(x, py, z, core)))
+        feat_copies.append(remote(src, dst, fs.at[2 + i], fr.at[2 + i], peer))
     partner = device(x, y, z, mate)
-    mate_copies = [remote(block, other.at[x], gs.at[0], gr.at[0], partner)]
-
-    def fill(row_block, columns, image, vectors, count):
-        scores = lax.dot_general(image, vectors, NT, preferred_element_type=F32)
-        rows = pl.ds(pl.multiple_of(row_block * BLOCK, BLOCK), count)
-        weights[rows, pl.ds(pl.multiple_of(columns * BLOCK, BLOCK), BLOCK)] = jnp.exp(
-            20.0 * scores
-        ).astype(BF16)
-
-    def fill_images(row_block, image, count):
-        for px in range(NX):
-            fill(row_block, core * NX + px, image, protos[px * NY + yl], count)
-            fill(row_block, mate * NX + px, image, other[px], count)
-
-    for slot, (copy, d) in enumerate(zip(proto_copies, (3, 1, 2))):
-        copy.wait_recv()
+    mate_copies = [remote(proto_ref, other.at[x], gs.at[0], gr.at[0], partner)]
+    signal(token_a, two_y + two_z + one_y)
+
+    def place(ref, block, values):
+        ref[pl.ds(pl.multiple_of(block * BLOCK, BLOCK), values.shape[0]), :] = values
+
+    def fill(block, count):
+        rows = pl.ds(pl.multiple_of(block * BLOCK, BLOCK), count)
+        for k in range(0, TILE, HALF):
+            scores = lax.dot_general(
+                unit_feats[rows, :], unit_protos[k:k + HALF, :], NT, preferred_element_type=F32
+            )
+            weights[rows, k:k + HALF] = jnp.exp(20.0 * scores).astype(BF16)
+
+    loads[0].wait()
+    own_feat[...] = unit_rows(loaded[...])
+    place(unit_feats, yl * 2, own_feat[mine, :])
+    loads[1].wait()
+    place(unit_protos, core * NX + x, unit_rows(protos[batch]))
+    for slot, d in ((1, 3), (2, 1), (0, 2)):
+        proto_copies[slot].wait_recv()
         arrived = protos.at[xs[d] * NY + yl]
         mate_copies.append(
-            remote(arrived, other.at[xs[d]], gs.at[1 + slot], gr.at[1 + slot], partner)
+            remote(arrived, other.at[xs[d]], gs.at[len(mate_copies)], gr.at[len(mate_copies)], partner)
         )
-    for copy in mate_copies:
+        place(unit_protos, core * NX + xs[d], unit_rows(arrived[...]))
+    pl.semaphore_wait(token_a, 6)
+    signal(token_b, two_y + two_z)
+    for copy, px in zip(mate_copies, (x, xs[3], xs[1], xs[2])):
         copy.wait_recv()
-    fill_images(yl * 2, feats[yl], HALF)
+        place(unit_protos, mate * NX + px, unit_rows(other[px]))
+    fill(yl * 2, HALF)
     for copy, shift in zip(feat_copies[:2], (3, 1)):
         copy.wait_recv()
         source = lax.rem(yl + shift, NY)
-        fill_images(source * 2, feats[source], HALF)
+        place(unit_feats, source * 2, unit_rows(feats[source]))
+        fill(source * 2, HALF)
     source = lax.rem(yl + 2, NY)
     for i, copy in enumerate(feat_copies[2:]):
         copy.wait_recv()
-        fill_images(source * 2 + i, feats[source, i * BLOCK:(i + 1) * BLOCK], BLOCK)
+        place(unit_feats, source * 2 + i, unit_rows(feats[source, i * BLOCK:(i + 1) * BLOCK]))
+        fill(source * 2 + i, BLOCK)
 
     tile_mask = lax.broadcasted_iota(jnp.int32, (8, TILE), 1) // BLOCK == lax.broadcasted_iota(
         jnp.int32, (8, TILE), 0
@@ -141,7 +164,7 @@
 
     def row_sums(factor):
         wide = jnp.where(tile_mask, jnp.concatenate([factor] * 8, axis=1), 0.0)
-        summed = lax.dot_general(split(wide), weights[...], NT, preferred_element_type=F32)
+        summed = jnp.dot(split(wide), across[...], preferred_element_type=F32)
         return fold(jnp.broadcast_to(jnp.sum(summed, axis=0, keepdims=True), (8, TILE)))
 
     def start(value, own, slots, send, recv, peers):
@@ -159,6 +182,15 @@
     for step in range(ITERS):
         part = column_sums(row_factor)
         copies = start(part, col_own.at[step], col_in.at[step], cs.at[step], cr.at[step], col_peers)
+        if step == 0:
+            for k in range(0, TILE, HALF):
+                for j in range(0, TILE, HALF):
+                    scores = lax.dot_general(
+                        unit_protos[k:k + HALF, :], unit_feats[j:j + HALF, :], NT,
+                        preferred_element_type=F32,
+                    )
+                    across[k:k + HALF, j:j + HALF] = jnp.exp(20.0 * scores).astype(BF16)
+            pl.semaphore_wait(token_b, 4)
         part = finish(part, col_in.at[step], copies)
         col_factor = 1.0 / part
         if step == 1:
@@ -203,7 +235,9 @@
             for copy in k_copies:
                 copy.wait_recv()
             for b in range(NX * NY):
-                scores = lax.dot_general(own_feat[...], protos[b], NT, preferred_element_type=F32)
+                scores = lax.dot_general(
+                    own_feat[...], unit_rows(protos[b]), NT, preferred_element_type=F32
+                )
                 factor = col_last[b % NY, b // NY:b // NY + 1, :]
                 scaled_ref[:, b * BLOCK:(b + 1) * BLOCK] = jnp.exp(20.0 * scores) * factor
             row_ref[...] = 1.0 / finish(part, lastz_in, copies)
@@ -233,6 +267,7 @@
 
 def local(features, prototypes):
     vmem = pl.BlockSpec(memory_space=pltpu.VMEM)
+    hbm = pl.BlockSpec(memory_space=pltpu.HBM)
     dma = pltpu.SemaphoreType.DMA
     early = ITERS - 1
     scaled, rows = pl.pallas_call(
@@ -241,13 +276,17 @@
             jax.ShapeDtypeStruct((ROWS, COLS), F32),
             jax.ShapeDtypeStruct((4, BLOCK), F32),
         ),
-        in_specs=[vmem, vmem],
+        in_specs=[hbm, hbm],
         out_specs=(vmem, vmem),
         scratch_shapes=[
             pltpu.VMEM((ROWS, DEPTH), BF16),
+            pltpu.VMEM((ROWS, DEPTH), BF16),
             pltpu.VMEM((NY, HALF, DEPTH), BF16),
+            pltpu.VMEM((TILE, DEPTH), BF16),
             pltpu.VMEM((NX * NY, BLOCK, DEPTH), BF16),
             pltpu.VMEM((NX, BLOCK, DEPTH), BF16),
+            pltpu.VMEM((TILE, DEPTH), BF16),
+            pltpu.VMEM((TILE, TILE), BF16),
             pltpu.VMEM((TILE, TILE), BF16),
             pltpu.VMEM((ITERS, 8, BLOCK), BF16),
             pltpu.VMEM((ITERS, 7, 8, BLOCK), BF16),
@@ -264,11 +303,12 @@
             dma((ITERS, 7)), dma((ITERS, 7)), dma((early, 7)), dma((early, 7)),
             dma((early, 11)), dma((early, 11)), dma((15,)), dma((15,)), dma((11,)), dma((11,)),
             dma((3,)), dma((3,)), dma((3, 2)), dma((3, 2)), dma((3, 2)), dma((3, 2)), dma((3,)), dma((3,)),
+            dma((2,)), pltpu.SemaphoreType.REGULAR, pltpu.SemaphoreType.REGULAR,
         ],
         compiler_params=pltpu.CompilerParams(
             collective_id=0, has_side_effects=True, vmem_limit_bytes=24 << 20
         ),
-    )(features, prototypes)
+    )(*(pltpu.with_memory_space_constraint(array, pltpu.HBM) for array in (features, prototypes)))
     return (scaled * rows.reshape(ROWS)[:, None]).astype(BF16)
 
 

time: 78.2 us -> 73.3 us (0.937)
  Pallas kernels: 74.6 us -> 71.5 us
  local copies, waits for them, and re-layouts: 1.79 us -> 0 us
    pallas_call x1, Pallas kernels: 74.6 us -> 71.5 us  [local(): pl.pallas_call(kernel, out_shape=(jax.ShapeDtypeStruct((ROWS, COLS), F32)...]
    unnamed x4 -> x0, local copies, waits for them, and re-layouts: 1.79 us -> none
where the time goes in v3:
time: 73.3 us; the launch traced here: 73.2 us
  Pallas kernels  71.5 us (98%)
  other arithmetic  1.61 us (2%)
    pallas_call x1, Pallas kernels, local(): pl.pallas_call(kernel, out_shape=(jax.ShapeDtypeStruct((ROWS, COLS), F32)...  71.5 us
    convert_element_type x1, other arithmetic, local(): return (scaled * rows.reshape(ROWS)[:, None]).astype(BF16)  1.61 us

profile of v3, /device:TPU:1, one launch (start us, length us, event | category | flops | bytes accessed | tf_op | source)
XLA Modules:
  0.0 73.2 jit_solution(1378758709427764484)
XLA Ops:
  0.0 71.5 %shard_map.28 = (f32[512,2048]{1,0:T(8,128)S(1)}, f32[4,128]{1,0:T(4,128)S(1)}) custom-call(bf16[512,256]{1,0:T(8,128)(2,1)} %feat_ref.1, bf16[128,256]{1,0:T(8,128)(2,1)} %proto_ref.1), custom_call_target="tpu_custom_call" | custom-call | tf_op jit(solution)/shard_map/pallas_call | solution.py:273
  71.5 1.6 %multiply_convert_fusion = bf16[512,2048]{1,0:T(8,128)(2,1)} fusion(f32[512,2048]{1,0:T(8,128)S(1)} %get-tuple-element.7, f32[512]{0:T(512)S(1)} %bitcast.1), kind=kLoop, calls=%fused_computation | loop fusion | flops 2097152 | bytes 6293504 | tf_op jit(solution)/shard_map/convert_element_type | solution.py:312

commit v4 on v3

--- a/solution.py
+++ b/solution.py
@@ -9,6 +9,7 @@
 NX, NY, NZ, RING = 4, 4, 12, 8
 ROWS, COLS, DEPTH, BLOCK = 512, 2048, 256, 128
 TILE, HALF = 1024, 256
+PIECE = 64
 TOTAL_PROTOS = 98304.0
 MESH = pl.DeviceIdType.MESH
 NT = (((1,), (1,)), ((), ()))
@@ -34,21 +35,22 @@
     fs, fr, ps, pr, gs, gr, cs, cr, ys, yr, zs, zr, ls, lr, lzs, lzr, bs, br, es, er, hs, hr, ks, kr, ms, token_a, token_b,
 ):
     batch, proto = lax.axis_index("batch"), lax.axis_index("proto")
-    x, yl = batch // NY, lax.rem(batch, NY)
-    yh, z, core = proto // (2 * NZ), lax.rem(proto // 2, NZ), lax.rem(proto, 2)
+    x = lax.div(batch, NY)
+    yl = batch - NY * x
+    yh = lax.div(proto + 8, 32)
+    pair = lax.div(proto, 2)
+    z, core = pair - NZ * yh, proto - 2 * pair
     y = yh * NY + yl
     mate = 1 - core
 
     def device(px, py, pz, pcore):
-        return {
-            "batch": px * NY + lax.rem(py, NY),
-            "proto": ((py // NY) * NZ + pz) * 2 + pcore,
-        }
-
-    xs = [lax.rem(x + d, NX) for d in range(NX)]
-    ry = [lax.rem(y + d, RING) for d in range(RING)]
-    rz = [lax.rem(z + d, NZ) for d in range(NZ)]
-    near_y = [yl, yl + 1 - 2 * lax.rem(yl, 2), lax.rem(yl + 2, NY), NY - 1 - yl]
+        high = lax.div(py, NY)
+        return {"batch": (px - high) * NY + py, "proto": (high * NZ + pz) * 2 + pcore}
+
+    xs = [x] + [x + d - NX * lax.div(x + d, NX) for d in range(1, NX)]
+    ry = [y] + [y + d - RING * lax.div(y + d, RING) for d in range(1, RING)]
+    rz = [z] + [z + d - NZ * lax.div(z + d + 4, 16) for d in range(1, NZ)]
+    near_y = [yl, yl + 1 - 2 * (yl - 2 * lax.div(yl, 2)), yl + 2 - NY * lax.div(yl, 2), NY - 1 - yl]
     col_peers = [device(xs[d], y, z, c) for d in (2, 1, 3) for c in (core, mate)]
     col_peers.append(device(x, y, z, mate))
     far_y = [ry[d] for d in (4, 3, 5, 2, 6, 1, 7)]
@@ -92,14 +94,13 @@
         for d in (2, 1, 3)
     ]
     mine = pl.ds(pl.multiple_of(core * HALF, HALF), HALF)
-    feat_copies = [
-        remote(feat_ref.at[mine], feats.at[yl], fs.at[i], fr.at[i], peer)
-        for i, peer in enumerate(one_y)
-    ]
-    for i, peer in enumerate(two_y):
+    feat_copies = []
+    for i, peer in ((0, two_y[0]), (1, two_y[1]), (0, one_y[0]), (0, one_y[1]), (1, one_y[0]), (1, one_y[1])):
         src = feat_ref.at[pl.ds(pl.multiple_of(core * HALF + i * BLOCK, BLOCK), BLOCK)]
-        dst = feats.at[yl, pl.ds(i * BLOCK, BLOCK)]
-        feat_copies.append(remote(src, dst, fs.at[2 + i], fr.at[2 + i], peer))
+        slot = len(feat_copies)
+        feat_copies.append(
+            remote(src, feats.at[yl, pl.ds(i * BLOCK, BLOCK)], fs.at[slot], fr.at[slot], peer)
+        )
     partner = device(x, y, z, mate)
     mate_copies = [remote(proto_ref, other.at[x], gs.at[0], gr.at[0], partner)]
     signal(token_a, two_y + two_z + one_y)
@@ -133,14 +134,9 @@
         copy.wait_recv()
         place(unit_protos, mate * NX + px, unit_rows(other[px]))
     fill(yl * 2, HALF)
-    for copy, shift in zip(feat_copies[:2], (3, 1)):
-        copy.wait_recv()
-        source = lax.rem(yl + shift, NY)
-        place(unit_feats, source * 2, unit_rows(feats[source]))
-        fill(source * 2, HALF)
-    source = lax.rem(yl + 2, NY)
-    for i, copy in enumerate(feat_copies[2:]):
-        copy.wait_recv()
+    for slot, shift, i in ((0, 2, 0), (1, 2, 1), (2, 3, 0), (3, 1, 0), (4, 3, 1), (5, 1, 1)):
+        feat_copies[slot].wait_recv()
+        source = yl + shift - NY * lax.div(yl + shift, NY)
         place(unit_feats, source * 2 + i, unit_rows(feats[source, i * BLOCK:(i + 1) * BLOCK]))
         fill(source * 2 + i, BLOCK)
 
@@ -208,9 +204,9 @@
             last_col = jnp.where(core == 0, col_factor[:4], col_factor[4:]) * TOTAL_PROTOS
             col_last[yl] = last_col
             for k in range(4):
-                last_own[k] = part[2 * k:2 * k + 2]
+                last_own[k] = part[2 * k:2 * k + 2].astype(BF16)
             copies = [
-                remote(last_own.at[lax.rem(py, NY)], last_in.at[i], ls.at[i], lr.at[i], peer)
+                remote(last_own.at[py - NY * lax.div(py, NY)], last_in.at[i], ls.at[i], lr.at[i], peer)
                 for i, (py, peer) in enumerate(last_peers)
             ]
             k_copies = [
@@ -218,14 +214,14 @@
                        device(x, yh * NY + near_y[k], z, core))
                 for k in range(1, NY)
             ]
-            mine_sum = last_own[yl]
+            mine_sum = last_own[yl].astype(F32)
             mate_sum = jnp.zeros((2, BLOCK), F32)
             for i, copy in enumerate(copies):
                 copy.wait_recv()
                 if i < 7:
-                    mine_sum = mine_sum + last_in[i]
+                    mine_sum = mine_sum + last_in[i].astype(F32)
                 else:
-                    mate_sum = mate_sum + last_in[i]
+                    mate_sum = mate_sum + last_in[i].astype(F32)
             first = jnp.where(core == 0, mine_sum, mate_sum)
             second = jnp.where(core == 0, mate_sum, mine_sum)
             part = jnp.concatenate([first, second], axis=0)
@@ -240,7 +236,11 @@
                 )
                 factor = col_last[b % NY, b // NY:b // NY + 1, :]
                 scaled_ref[:, b * BLOCK:(b + 1) * BLOCK] = jnp.exp(20.0 * scores) * factor
+            for copy in sent[:-len(copies)]:
+                copy.wait_send()
             row_ref[...] = 1.0 / finish(part, lastz_in, copies)
+            for copy in copies:
+                copy.wait_send()
             break
         copies = start(part, ring_own.at[step], ring_in.at[step], ys.at[step], yr.at[step], ring_peers)
         part = finish(part, ring_in.at[step], copies)
@@ -261,8 +261,22 @@
                         remote(piece, piece, hs.at[k - 1, side], hr.at[k - 1, side], device(xs[d], y, z, core))
                     )
         row_factor = 1.0 / finish(part, z_in.at[step], copies)
-    for copy in sent:
-        copy.wait_send()
+
+
+def scale_rows(scaled_ref, row_ref, out_ref, rounded, sems):
+    copies = []
+    for k in range(ROWS // BLOCK):
+        column = jnp.broadcast_to(row_ref[k:k + 1, :], (BLOCK, BLOCK)).T
+        for first in range(0, BLOCK, PIECE):
+            rows = pl.ds(k * BLOCK + first, PIECE)
+            factor = jnp.concatenate([column[first:first + PIECE]] * (COLS // BLOCK), axis=1)
+            rounded[rows, :] = (scaled_ref[rows, :] * factor).astype(BF16)
+            copies.append(
+                pltpu.make_async_copy(rounded.at[rows], out_ref.at[rows], sems.at[len(copies)])
+            )
+            copies[-1].start()
+    for copy in copies:
+        copy.wait()
 
 
 def local(features, prototypes):
@@ -294,12 +308,12 @@
             pltpu.VMEM((early, 7, 8, BLOCK), BF16),
             pltpu.VMEM((early, 8, BLOCK), BF16),
             pltpu.VMEM((early, 11, 8, BLOCK), BF16),
-            pltpu.VMEM((NY, 2, BLOCK), F32),
-            pltpu.VMEM((15, 2, BLOCK), F32),
-            pltpu.VMEM((4, BLOCK), F32),
-            pltpu.VMEM((11, 4, BLOCK), F32),
+            pltpu.VMEM((NY, 2, BLOCK), BF16),
+            pltpu.VMEM((15, 2, BLOCK), BF16),
+            pltpu.VMEM((4, BLOCK), BF16),
+            pltpu.VMEM((11, 4, BLOCK), BF16),
             pltpu.VMEM((NY, NX, BLOCK), F32),
-            dma((4,)), dma((4,)), dma((3,)), dma((3,)), dma((4,)), dma((4,)),
+            dma((6,)), dma((6,)), dma((3,)), dma((3,)), dma((4,)), dma((4,)),
             dma((ITERS, 7)), dma((ITERS, 7)), dma((early, 7)), dma((early, 7)),
             dma((early, 11)), dma((early, 11)), dma((15,)), dma((15,)), dma((11,)), dma((11,)),
             dma((3,)), dma((3,)), dma((3, 2)), dma((3, 2)), dma((3, 2)), dma((3, 2)), dma((3,)), dma((3,)),
@@ -309,7 +323,15 @@
             collective_id=0, has_side_effects=True, vmem_limit_bytes=24 << 20
         ),
     )(*(pltpu.with_memory_space_constraint(array, pltpu.HBM) for array in (features, prototypes)))
-    return (scaled * rows.reshape(ROWS)[:, None]).astype(BF16)
+    pieces = ROWS // PIECE
+    return pl.pallas_call(
+        scale_rows,
+        out_shape=jax.ShapeDtypeStruct((ROWS, COLS), BF16),
+        in_specs=[vmem, vmem],
+        out_specs=pl.BlockSpec(memory_space=pltpu.HBM),
+        scratch_shapes=[pltpu.VMEM((ROWS, COLS), BF16), dma((pieces,))],
+        compiler_params=pltpu.CompilerParams(vmem_limit_bytes=16 << 20),
+    )(scaled, rows)
 
 
 def solution(mesh):

time: 73.3 us -> 72.4 us (0.988)
  other arithmetic: 1.61 us -> 0 us
  Pallas kernels: 71.5 us -> 72.3 us
    convert_element_type x1 -> x0, other arithmetic: 1.61 us -> none  [local(): return (scaled * rows.reshape(ROWS)[:, None]).astype(BF16)]
    pallas_call x0 -> x1, Pallas kernels: none -> 1.5 us  [local(): pl.pallas_call(scale_rows, out_shape=jax.ShapeDtypeStruct((ROWS, COLS), B...]
    pallas_call x1, Pallas kernels: 71.5 us -> 70.8 us  [local(): pl.pallas_call(kernel, out_shape=(jax.ShapeDtypeStruct((ROWS, COLS), F32)...]
where the time goes in v4:
time: 72.4 us; the launch traced here: 72.3 us
  Pallas kernels  72.3 us (100%)
    pallas_call x1, Pallas kernels, local(): pl.pallas_call(kernel, out_shape=(jax.ShapeDtypeStruct((ROWS, COLS), F32)...  70.8 us
    pallas_call x1, Pallas kernels, local(): pl.pallas_call(scale_rows, out_shape=jax.ShapeDtypeStruct((ROWS, COLS), B...  1.5 us

profile of v4, /device:TPU:1, one launch (start us, length us, event | category | flops | bytes accessed | tf_op | source)
XLA Modules:
  0.0 72.3 jit_solution(4264614499391800941)
XLA Ops:
  0.0 70.8 %shard_map.28 = (f32[512,2048]{1,0:T(8,128)S(1)}, f32[4,128]{1,0:T(4,128)S(1)}) custom-call(bf16[512,256]{1,0:T(8,128)(2,1)} %feat_ref.1, bf16[128,256]{1,0:T(8,128)(2,1)} %proto_ref.1), custom_call_target="tpu_custom_call" | custom-call | tf_op jit(solution)/shard_map/pallas_call | solution.py:287
  70.8 1.5 %shard_map.29 = bf16[512,2048]{1,0:T(8,128)(2,1)} custom-call(f32[512,2048]{1,0:T(8,128)S(1)} %get-tuple-element.7.scaled_ref, f32[4,128]{1,0:T(4,128)S(1)} %get-tuple-element.8.row_ref), custom_call_target="tpu_custom_call" | custom-call | tf_op jit(solution)/shard_map/pallas_call | solution.py:327

commit v5 on v4

--- a/solution.py
+++ b/solution.py
@@ -32,7 +32,8 @@
     feat_ref, proto_ref, scaled_ref, row_ref,
     loaded, own_feat, feats, unit_feats, protos, other, unit_protos, weights, across,
     col_own, col_in, ring_own, ring_in, z_own, z_in, last_own, last_in, lastz_own, lastz_in, col_last,
-    fs, fr, ps, pr, gs, gr, cs, cr, ys, yr, zs, zr, ls, lr, lzs, lzr, bs, br, es, er, hs, hr, ks, kr, ms, token_a, token_b,
+    fs, fr, ps, pr, gs, gr, cs, cr, ys, yr, zs, zr, ls, lr, lzs, lzr, bs, br, es, er, hs, hr, ks, kr, ms, token_a, token_b, totals,
+    far_in, ds, dr,
 ):
     batch, proto = lax.axis_index("batch"), lax.axis_index("proto")
     x = lax.div(batch, NY)
@@ -58,6 +59,7 @@
     last_peers = [(py, device(x, py, z, core)) for py in far_y]
     last_peers += [(py, device(x, py, z, mate)) for py in far_y + [y]]
     z_peers = [device(x, y, rz[d], core) for d in (6, 5, 7, 4, 8, 3, 9, 2, 10, 1, 11)]
+    far_peers = [device(x, py, rz[6], core) for py in far_y + [y]]
 
     def signal(semaphore, peers):
         for peer in peers:
@@ -108,13 +110,19 @@
     def place(ref, block, values):
         ref[pl.ds(pl.multiple_of(block * BLOCK, BLOCK), values.shape[0]), :] = values
 
-    def fill(block, count):
+    totals[...] = jnp.zeros_like(totals)
+    ours, theirs = (core * NX, core * NX + 2), (mate * NX, mate * NX + 2)
+
+    def fill(block, count, pairs):
         rows = pl.ds(pl.multiple_of(block * BLOCK, BLOCK), count)
-        for k in range(0, TILE, HALF):
+        for pair in pairs:
+            columns = pl.ds(pl.multiple_of(pair * BLOCK, HALF), HALF)
             scores = lax.dot_general(
-                unit_feats[rows, :], unit_protos[k:k + HALF, :], NT, preferred_element_type=F32
+                unit_feats[rows, :], unit_protos[columns, :], NT, preferred_element_type=F32
             )
-            weights[rows, k:k + HALF] = jnp.exp(20.0 * scores).astype(BF16)
+            values = jnp.exp(20.0 * scores)
+            weights[rows, columns] = values.astype(BF16)
+            totals[:, columns] += jnp.sum(values.reshape(count // 8, 8, HALF), axis=0)
 
     loads[0].wait()
     own_feat[...] = unit_rows(loaded[...])
@@ -130,15 +138,24 @@
         place(unit_protos, core * NX + xs[d], unit_rows(arrived[...]))
     pl.semaphore_wait(token_a, 6)
     signal(token_b, two_y + two_z)
+    def take(slot, source, i):
+        feat_copies[slot].wait_recv()
+        place(unit_feats, source * 2 + i, unit_rows(feats[source, i * BLOCK:(i + 1) * BLOCK]))
+
+    fill(yl * 2, HALF, ours)
+    source = yl + 2 - NY * lax.div(yl + 2, NY)
+    take(0, source, 0)
+    take(1, source, 1)
+    fill(source * 2, HALF, ours)
     for copy, px in zip(mate_copies, (x, xs[3], xs[1], xs[2])):
         copy.wait_recv()
         place(unit_protos, mate * NX + px, unit_rows(other[px]))
-    fill(yl * 2, HALF)
-    for slot, shift, i in ((0, 2, 0), (1, 2, 1), (2, 3, 0), (3, 1, 0), (4, 3, 1), (5, 1, 1)):
-        feat_copies[slot].wait_recv()
+    fill(yl * 2, HALF, theirs)
+    fill(source * 2, HALF, theirs)
+    for slot, shift, i in ((2, 3, 0), (3, 1, 0), (4, 3, 1), (5, 1, 1)):
         source = yl + shift - NY * lax.div(yl + shift, NY)
-        place(unit_feats, source * 2 + i, unit_rows(feats[source, i * BLOCK:(i + 1) * BLOCK]))
-        fill(source * 2 + i, BLOCK)
+        take(slot, source, i)
+        fill(source * 2 + i, BLOCK, ours + theirs)
 
     tile_mask = lax.broadcasted_iota(jnp.int32, (8, TILE), 1) // BLOCK == lax.broadcasted_iota(
         jnp.int32, (8, TILE), 0
@@ -174,9 +191,12 @@
         return total
 
     half = BLOCK // 2
-    row_factor = jnp.ones((8, BLOCK), F32)
     for step in range(ITERS):
-        part = column_sums(row_factor)
+        if step:
+            part = column_sums(row_factor)
+        else:
+            summed = jnp.sum(totals[...], axis=0, keepdims=True)
+            part = fold(jnp.broadcast_to(summed, (8, TILE)))
         copies = start(part, col_own.at[step], col_in.at[step], cs.at[step], cr.at[step], col_peers)
         if step == 0:
             for k in range(0, TILE, HALF):
@@ -243,8 +263,15 @@
                 copy.wait_send()
             break
         copies = start(part, ring_own.at[step], ring_in.at[step], ys.at[step], yr.at[step], ring_peers)
+        far_copies = []
+        if step:
+            far_copies = [
+                remote(ring_own.at[step], far_in.at[i], ds.at[i], dr.at[i], peer)
+                for i, peer in enumerate(far_peers)
+            ]
         part = finish(part, ring_in.at[step], copies)
-        copies = start(part, z_own.at[step], z_in.at[step], zs.at[step], zr.at[step], z_peers)
+        peers = z_peers[1:] if step else z_peers
+        copies = start(part, z_own.at[step], z_in.at[step], zs.at[step], zr.at[step], peers)
         if step == 0:
             block = protos.at[batch]
             y_copies = [
@@ -260,7 +287,8 @@
                     f_copies.append(
                         remote(piece, piece, hs.at[k - 1, side], hr.at[k - 1, side], device(xs[d], y, z, core))
                     )
-        row_factor = 1.0 / finish(part, z_in.at[step], copies)
+        part = finish(part, z_in.at[step], copies)
+        row_factor = 1.0 / finish(part, far_in, far_copies)
 
 
 def scale_rows(scaled_ref, row_ref, out_ref, rounded, sems):
@@ -318,6 +346,8 @@
             dma((early, 11)), dma((early, 11)), dma((15,)), dma((15,)), dma((11,)), dma((11,)),
             dma((3,)), dma((3,)), dma((3, 2)), dma((3, 2)), dma((3, 2)), dma((3, 2)), dma((3,)), dma((3,)),
             dma((2,)), pltpu.SemaphoreType.REGULAR, pltpu.SemaphoreType.REGULAR,
+            pltpu.VMEM((8, TILE), F32),
+            pltpu.VMEM((8, 8, BLOCK), BF16), dma((8,)), dma((8,)),
         ],
         compiler_params=pltpu.CompilerParams(
             collective_id=0, has_side_effects=True, vmem_limit_bytes=24 << 20

time: 72.4 us -> 71.8 us (level)
  no operation moved by 1% of the time
where the time goes in v5:
time: 71.8 us; the launch traced here: 71.7 us
  Pallas kernels  71.7 us (100%)
    pallas_call x1, Pallas kernels, local(): pl.pallas_call(kernel, out_shape=(jax.ShapeDtypeStruct((ROWS, COLS), F32)...  70.2 us
    pallas_call x1, Pallas kernels, local(): pl.pallas_call(scale_rows, out_shape=jax.ShapeDtypeStruct((ROWS, COLS), B...  1.5 us

profile of v5, /device:TPU:1, one launch (start us, length us, event | category | flops | bytes accessed | tf_op | source)
XLA Modules:
  0.0 71.7 jit_solution(15102859814176505723)
XLA Ops:
  0.0 70.2 %shard_map.28 = (f32[512,2048]{1,0:T(8,128)S(1)}, f32[4,128]{1,0:T(4,128)S(1)}) custom-call(bf16[512,256]{1,0:T(8,128)(2,1)} %feat_ref.1, bf16[128,256]{1,0:T(8,128)(2,1)} %proto_ref.1), custom_call_target="tpu_custom_call" | custom-call | tf_op jit(solution)/shard_map/pallas_call | solution.py:315
  70.2 1.5 %shard_map.29 = bf16[512,2048]{1,0:T(8,128)(2,1)} custom-call(f32[512,2048]{1,0:T(8,128)S(1)} %get-tuple-element.7.scaled_ref, f32[4,128]{1,0:T(4,128)S(1)} %get-tuple-element.8.row_ref), custom_call_target="tpu_custom_call" | custom-call | tf_op jit(solution)/shard_map/pallas_call | solution.py:357

commit v6 on v5

--- a/solution.py
+++ b/solution.py
@@ -49,26 +49,23 @@
         return {"batch": (px - high) * NY + py, "proto": (high * NZ + pz) * 2 + pcore}
 
     xs = [x] + [x + d - NX * lax.div(x + d, NX) for d in range(1, NX)]
-    ry = [y] + [y + d - RING * lax.div(y + d, RING) for d in range(1, RING)]
-    rz = [z] + [z + d - NZ * lax.div(z + d + 4, 16) for d in range(1, NZ)]
-    near_y = [yl, yl + 1 - 2 * (yl - 2 * lax.div(yl, 2)), yl + 2 - NY * lax.div(yl, 2), NY - 1 - yl]
+
+    def ring_at(d):
+        return y + d - RING * lax.div(y + d, RING)
+
+    def z_at(d):
+        return z + d - NZ * lax.div(z + d + 4, 16)
+
     col_peers = [device(xs[d], y, z, c) for d in (2, 1, 3) for c in (core, mate)]
     col_peers.append(device(x, y, z, mate))
-    far_y = [ry[d] for d in (4, 3, 5, 2, 6, 1, 7)]
-    ring_peers = [device(x, py, z, core) for py in far_y]
-    last_peers = [(py, device(x, py, z, core)) for py in far_y]
-    last_peers += [(py, device(x, py, z, mate)) for py in far_y + [y]]
-    z_peers = [device(x, y, rz[d], core) for d in (6, 5, 7, 4, 8, 3, 9, 2, 10, 1, 11)]
-    far_peers = [device(x, py, rz[6], core) for py in far_y + [y]]
-
     def signal(semaphore, peers):
         for peer in peers:
             pl.semaphore_signal(semaphore, inc=1, device_id=peer, device_id_type=MESH)
 
-    two_y = [device(x, py, z, core) for py in (ry[2], ry[6])]
-    one_y = [device(x, py, z, core) for py in (ry[1], ry[7])]
-    two_z = [device(x, y, pz, core) for pz in (rz[2], rz[10])]
-    one_z = [device(x, y, pz, core) for pz in (rz[1], rz[11])]
+    two_y = [device(x, py, z, core) for py in (ring_at(2), ring_at(6))]
+    one_y = [device(x, py, z, core) for py in (ring_at(1), ring_at(7))]
+    two_z = [device(x, y, pz, core) for pz in (z_at(2), z_at(10))]
+    one_z = [device(x, y, pz, core) for pz in (z_at(1), z_at(11))]
     barrier = pltpu.get_barrier_semaphore()
     partners = two_y + two_z + col_peers + one_y + one_z
     signal(barrier, partners)
@@ -106,6 +103,14 @@
     partner = device(x, y, z, mate)
     mate_copies = [remote(proto_ref, other.at[x], gs.at[0], gr.at[0], partner)]
     signal(token_a, two_y + two_z + one_y)
+
+    near_y = [yl, yl + 1 - 2 * (yl - 2 * lax.div(yl, 2)), yl + 2 - NY * lax.div(yl, 2), NY - 1 - yl]
+    far_y = [ring_at(d) for d in (4, 3, 5, 2, 6, 1, 7)]
+    ring_peers = [device(x, py, z, core) for py in far_y]
+    last_peers = [(py, device(x, py, z, core)) for py in far_y]
+    last_peers += [(py, device(x, py, z, mate)) for py in far_y + [y]]
+    z_peers = [device(x, y, z_at(d), core) for d in (6, 5, 7, 4, 8, 3, 9, 2, 10, 1, 11)]
+    far_peers = [device(x, py, z_at(6), core) for py in far_y + [y]]
 
     def place(ref, block, values):
         ref[pl.ds(pl.multiple_of(block * BLOCK, BLOCK), values.shape[0]), :] = values

time: 71.8 us -> 71.7 us (level)
  no operation moved by 1% of the time
where the time goes in v6:
time: 71.7 us; the launch traced here: 71.6 us
  Pallas kernels  71.6 us (100%)
    pallas_call x1, Pallas kernels, local(): pl.pallas_call(kernel, out_shape=(jax.ShapeDtypeStruct((ROWS, COLS), F32)...  70.1 us
    pallas_call x1, Pallas kernels, local(): pl.pallas_call(scale_rows, out_shape=jax.ShapeDtypeStruct((ROWS, COLS), B...  1.5 us

profile of v6, /device:TPU:1, one launch (start us, length us, event | category | flops | bytes accessed | tf_op | source)
XLA Modules:
  0.0 71.6 jit_solution(5650230511697320057)
XLA Ops:
  0.0 70.1 %shard_map.28 = (f32[512,2048]{1,0:T(8,128)S(1)}, f32[4,128]{1,0:T(4,128)S(1)}) custom-call(bf16[512,256]{1,0:T(8,128)(2,1)} %feat_ref.1, bf16[128,256]{1,0:T(8,128)(2,1)} %proto_ref.1), custom_call_target="tpu_custom_call" | custom-call | tf_op jit(solution)/shard_map/pallas_call | solution.py:320
  70.1 1.5 %shard_map.29 = bf16[512,2048]{1,0:T(8,128)(2,1)} custom-call(f32[512,2048]{1,0:T(8,128)S(1)} %get-tuple-element.7.scaled_ref, f32[4,128]{1,0:T(4,128)S(1)} %get-tuple-element.8.row_ref), custom_call_target="tpu_custom_call" | custom-call | tf_op jit(solution)/shard_map/pallas_call | solution.py:362
